TPU v7x, 32 devices: a whole 2x2x4 slice. The times are simulated.
32 devices in a mesh: seq: 16 (over z, x, core), head: 2 (over y).
Axes of the slice: x: 2, y: 2, z: 4, core: 2. Of those that a mesh axis runs over, the one named last changes fastest.
Arguments:
- queries: bfloat16 [2, 1024, 4096], P(None, ('seq', 'head')), may hold values from -6 to 6
- keys: bfloat16 [2, 1024, 4096], P(None, ('seq', 'head')), may hold values from -6 to 6
- values: bfloat16 [2, 1024, 4096], P(None, ('seq', 'head')), may hold values from -6 to 6
- rates: bfloat16 [2, 1024, 8], P(None, ('seq', 'head')), may hold values from 0.049804688 to 1
- fast_init: float32 [8, 3, 512, 256], P('head', None, 'seq'), may hold values from -0.25 to 0.25
Outputs:
- outputs: bfloat16 [2, 1024, 4096], P(None, 'seq', 'head')
All inputs are finite; a program needn't handle non-finite values.
Results may differ from a plain program's by a relative error of at most 0.0085.
Values may be sent and summed in bfloat16 or wider, within the bound.
No kernel may reach another device: no remote copies, remote signals or barrier semaphores. Data moves between devices by JAX's collectives and lax.ppermute only.
A program may use at most 64 MiB of HBM per device.

v0:
```python
import jax
import jax.numpy as jnp
from jax import lax
from jax.sharding import PartitionSpec as P

EPSILON = 1e-06
COEF_A = 3.4445
COEF_B = -4.775
COEF_C = 2.0315
LEARNING_STEP = 0.5
FULL_PRECISION = lax.Precision.HIGHEST


def silu_parts(gate_pre):
    sigmoid_value = jax.nn.sigmoid(gate_pre)
    return (gate_pre * sigmoid_value, sigmoid_value * (1.0 + gate_pre * (1.0 - sigmoid_value)))


def local_gram(weight_matrices):
    return jnp.einsum("hmrf,hmrg->hmfg", weight_matrices, weight_matrices, precision=FULL_PRECISION)


def newton_schulz(gradients, gram_fn):
    gram_matrix = gram_fn(gradients)
    norm_value = jnp.sqrt(jnp.trace(gram_matrix, axis1=2, axis2=3)) + EPSILON
    current_weights = gradients / norm_value[:, :, None, None]
    gram_matrix = gram_matrix / (norm_value * norm_value)[:, :, None, None]
    identity = jnp.eye(gram_matrix.shape[-1], dtype=gram_matrix.dtype)
    for sweeps in range(2):
        if sweeps > 0:
            gram_matrix = gram_fn(current_weights)
        square = jnp.einsum("hmfg,hmgk->hmfk", gram_matrix, gram_matrix, precision=FULL_PRECISION)
        polynomial_update = COEF_A * identity + COEF_B * gram_matrix + COEF_C * square
        current_weights = jnp.einsum(
            "hmrf,hmfg->hmrg", current_weights, polynomial_update, precision=FULL_PRECISION
        )
    return current_weights


def local(queries, keys, values, rates, fast_init):
    weights = lax.all_gather(fast_init, "seq", axis=2, tiled=True)
    head_count = weights.shape[0]
    head_size = weights.shape[2]
    results = []
    for group_index in range(queries.shape[0]):
        query_flat, key_flat, value_flat, rate_rows = (
            lax.all_to_all(queries[group_index], "head", split_axis=1, concat_axis=0, tiled=True),
            lax.all_to_all(keys[group_index], "head", split_axis=1, concat_axis=0, tiled=True),
            lax.all_to_all(values[group_index], "head", split_axis=1, concat_axis=0, tiled=True),
            lax.all_to_all(rates[group_index], "head", split_axis=1, concat_axis=0, tiled=True),
        )
        row_count = query_flat.shape[0]
        query_rows = query_flat.reshape(row_count, head_count, head_size)
        key_rows = key_flat.reshape(row_count, head_count, head_size)
        value_rows = value_flat.reshape(row_count, head_count, head_size)
        low = weights.astype(jnp.bfloat16)
        gate_pre = jnp.einsum(
            "rhd,hdf->rhf", key_rows, low[:, 0], preferred_element_type=jnp.float32
        )
        up_proj = jnp.einsum(
            "rhd,hdf->rhf", key_rows, low[:, 1], preferred_element_type=jnp.float32
        )
        activated_hidden, slope_value = silu_parts(gate_pre)
        hidden = (activated_hidden * up_proj).astype(jnp.bfloat16)
        out_grad = (
            -(rate_rows.astype(jnp.float32)[:, :, None] * value_rows.astype(jnp.float32))
        ).astype(jnp.bfloat16)
        hidden_grad = jnp.einsum(
            "rhd,hdf->rhf", out_grad, low[:, 2], preferred_element_type=jnp.float32
        )
        gate_grad = (hidden_grad * up_proj * slope_value).astype(jnp.bfloat16)
        up_grad = (hidden_grad * activated_hidden).astype(jnp.bfloat16)
        gradients = jnp.stack(
            [
                jnp.einsum("rhd,rhf->hdf", key_rows, gate_grad, preferred_element_type=jnp.float32),
                jnp.einsum("rhd,rhf->hdf", key_rows, up_grad, preferred_element_type=jnp.float32),
                jnp.einsum("rhd,rhf->hdf", out_grad, hidden, preferred_element_type=jnp.float32),
            ],
            axis=1,
        )
        total_grad = lax.psum(gradients, "seq")
        update = newton_schulz(total_grad, local_gram)
        weights = weights - LEARNING_STEP * update
        low = weights.astype(jnp.bfloat16)
        query_gate = jnp.einsum(
            "rhd,hdf->rhf", query_rows, low[:, 0], preferred_element_type=jnp.float32
        )
        query_up = jnp.einsum(
            "rhd,hdf->rhf", query_rows, low[:, 1], preferred_element_type=jnp.float32
        )
        query_act, unused_slope = silu_parts(query_gate)
        query_hidden = (query_act * query_up).astype(jnp.bfloat16)
        result = jnp.einsum(
            "rhf,hdf->rhd", query_hidden, low[:, 2], preferred_element_type=jnp.float32
        )
        results.append(result.astype(jnp.bfloat16).reshape(row_count, head_count * head_size))
    return jnp.stack(results)


def solution(mesh):
    return jax.shard_map(
        local,
        mesh=mesh,
        in_specs=(
            P(None, ("seq", "head"), None),
            P(None, ("seq", "head"), None),
            P(None, ("seq", "head"), None),
            P(None, ("seq", "head"), None),
            P("head", None, "seq", None),
        ),
        out_specs=P(None, "seq", "head"),
        check_vma=False,
    )
```

profile of v0, /device:TPU:0, one launch (start us, length us, event | category | flops | bytes accessed | tf_op | source)
XLA Modules:
  0.0 496.7 jit_solution(14485534307048518920)
XLA Ops:
  6.5 1.8 copy.62
  8.4 1.3 fusion.99
  9.7 4.3 all-to-all-start
  16.0 1.7 all-to-all-done
  17.7 3.5 all-to-all-start.2
  22.2 4.1 all-to-all-done.2
  26.4 3.4 all-to-all-start.1
  30.1 4.8 all-to-all-done.1
  35.5 38.2 %all-gather.2.cloned.1.call-done = f32[4,3,512,256]{3,2,0,1:T(8,128)} async-done(((f32[4,3,32,256]{3,2,0,1:T(8,128)}), f32[4,3,512,256]{3,2,0,1:T(8,128)}) %all-gather.2.cloned.1.call-update) | async-done | bytes 6291472 | tf_op jit(solution)/shard_map/all_gather | solution.py:41
  73.7 3.1 convert_element_type.105
  79.3 3.3 pad_maximum_fusion
  82.6 3.2 all-to-all-start.4
  87.8 1.6 all-to-all-done.4
  89.5 3.4 all-to-all-start.5
  93.0 5.1 %all-to-all-done.5 = bf16[32,2,2048]{2,0,1:T(8,128)(2,1)S(1)} async-done(((bf16[32,2,2048]{2,0,1:T(8,128)(2,1)}), bf16[32,2,2048]{2,0,1:T(8,128)(2,1)S(1)}, u32[]{:S(2)}, u32[]{:S(2)}) %all-to-all-start.5) | async-done | bytes 262176 | tf_op jit(solution)/shard_map/all_to_all | solution.py:49
  98.1 3.4 all-to-all-start.6
  102.2 4.5 all-to-all-done.6
  108.5 112.3 %all-reduce.3.cloned.1.call-done = f32[4,3,512,256]{2,3,0,1:T(8,128)} async-done(((f32[4,3,512,256]{2,3,0,1:T(8,128)}), f32[4,3,512,256]{2,3,0,1:T(8,128)}) %all-reduce.3.cloned.1.call-update) | async-done | bytes 6291472 | tf_op jit(solution)/shard_map/psum | solution.py:81
  220.8 19.0 %select_reduce_fusion.1 = (f32[4,3]{1,0:T(4,128)S(1)}, f32[4,3,256,256]{3,2,1,0:T(8,128)}) fusion(pred[256,256]{1,0:T(8,128)(4,1)S(1)} %iota_compare_fusion, f32[4,3,512,256]{2,3,0,1:T(8,128)} %all-reduce.3.cloned.1.call-done), kind=kOutput, calls=%fused_computation.31 | convolution fusion | flops 4833411072 | bytes 9502768 | tf_op jit(solution)/shard_map/hmrf,hmrg->hmfg/dot_general | solution.py:20
  239.9 6.4 %fusion.36 = f32[4,3,256,256]{3,2,1,0:T(8,128)S(1)} fusion(f32[4,3,256,256]{3,2,1,0:T(8,128)} %get-tuple-element.18, f32[4,3]{1,0:T(4,128)S(1)} %get-tuple-element.15), kind=kOutput, calls=%fused_computation.46 | convolution fusion | flops 2416705536 | bytes 6291504 | tf_op jit(solution)/shard_map/hmfg,hmgk->hmfk/dot_general | solution.py:32
  246.4 10.8 %fusion.2 = f32[4,3,512,256]{3,2,1,0:T(8,128)S(1)} fusion(f32[4,3,256,256]{3,2,1,0:T(8,128)S(1)} %fusion.36, f32[256,256]{1,0:T(8,128)S(1)} %broadcast_select_fusion, f32[4,3,256,256]{3,2,1,0:T(8,128)S(1)} %copy-done.1, f32[4,3]{1,0:T(4,128)S(1)} %get-tuple-element.15, f32[4,3,512,256]{2,3,0,1:T(8,128)S(1)} %bitcast.117, f32[4,3]{0,1:T(4,128)S(1)} %copy.76), kind=kOutput, calls=%fused_computation.4 | convolution fusion | flops 4837343232 | bytes 19136608 | tf_op jit(solution)/shard_map/hmrf,hmfg->hmrg/dot_general | solution.py:34
  257.2 10.6 %fusion.101 = f32[4,3,256,256]{3,2,1,0:T(8,128)S(1)} fusion(f32[4,3,512,256]{3,2,1,0:T(8,128)S(1)} %fusion.2), kind=kOutput, calls=%fused_computation.145 | convolution fusion | flops 4831838208 | bytes 9437184 | tf_op jit(solution)/shard_map/hmrf,hmrg->hmfg/dot_general | solution.py:20
  267.9 3.9 multiply_add_fusion.1
  271.8 8.1 %fusion.100 = (bf16[4,3,512,256]{3,2,0,1:T(8,128)(2,1)S(1)}, f32[4,3,512,256]{3,2,0,1:T(8,128)}) fusion(f32[4,3,512,256]{3,2,0,1:T(8,128)S(1)} %bitcast.115, f32[4,3,256,256]{3,2,1,0:T(8,128)S(1)} %multiply_add_fusion.1, f32[4,3,512,256]{3,2,1,0:T(8,128)S(1)} %fusion.2), kind=kOutput, calls=%fused_computation.144 | convolution fusion | flops 4836556800 | bytes 25165824 | tf_op jit(solution)/shard_map/hmrf,hmfg->hmrg/dot_general | solution.py:34
  282.6 3.3 pad_maximum_fusion.1
  286.0 1.9 fusion.96
  287.9 1.9 all_to_all.95
  289.7 1.7 copy.80
  291.5 4.1 all-to-all-start.3
  295.6 1.9 all_to_all.105
  297.4 1.7 copy.101
  299.1 1.7 all-to-all-done.3
  300.9 4.1 all-to-all-start.7
  305.0 1.9 reshape.93
  306.8 3.4 all-to-all-done.7
  310.2 1.8 reshape.95
  312.1 2.0 convolution_bitcast_fusion.12
  314.0 2.4 fusion.38
  316.4 1.2 copy.83
  318.4 107.0 %all-reduce.5.cloned.1.call-done = f32[4,3,512,256]{2,3,0,1:T(8,128)} async-done(((f32[4,3,512,256]{2,3,0,1:T(8,128)}), f32[4,3,512,256]{2,3,0,1:T(8,128)}) %all-reduce.5.cloned.1.call-update) | async-done | bytes 6291472 | tf_op jit(solution)/shard_map/psum | solution.py:81
  425.5 18.8 %select_reduce_fusion = (f32[4,3]{1,0:T(4,128)S(1)}, f32[4,3,256,256]{3,2,1,0:T(8,128)}) fusion(pred[256,256]{1,0:T(8,128)(4,1)S(1)} %iota_compare_fusion, f32[4,3,512,256]{2,3,0,1:T(8,128)} %all-reduce.5.cloned.1.call-done), kind=kOutput, calls=%fused_computation.24 | convolution fusion | flops 4833411072 | bytes 9502768 | tf_op jit(solution)/shard_map/hmrf,hmrg->hmfg/dot_general | solution.py:20
  444.4 6.7 %fusion.37 = f32[4,3,256,256]{3,2,1,0:T(8,128)S(1)} fusion(f32[4,3,256,256]{3,2,1,0:T(8,128)} %get-tuple-element.22, f32[4,3]{1,0:T(4,128)S(1)} %get-tuple-element.13), kind=kOutput, calls=%fused_computation.47 | convolution fusion | flops 2416705536 | bytes 6291504 | tf_op jit(solution)/shard_map/hmfg,hmgk->hmfk/dot_general | solution.py:32
  451.1 11.4 %fusion = f32[4,3,512,256]{3,2,1,0:T(8,128)S(1)} fusion(f32[4,3,256,256]{3,2,1,0:T(8,128)S(1)} %fusion.37, f32[256,256]{1,0:T(8,128)S(1)} %broadcast_select_fusion, f32[4,3,256,256]{3,2,1,0:T(8,128)S(1)} %copy-done, f32[4,3]{1,0:T(4,128)S(1)} %get-tuple-element.13, f32[4,3,512,256]{2,3,0,1:T(8,128)S(1)} %bitcast.119, f32[4,3]{0,1:T(4,128)S(1)} %copy.97), kind=kOutput, calls=%fused_computation.2 | convolution fusion | flops 4837343232 | bytes 19136608 | tf_op jit(solution)/shard_map/hmrf,hmfg->hmrg/dot_general | solution.py:34
  462.6 10.8 %fusion.102 = f32[4,3,256,256]{3,2,1,0:T(8,128)S(1)} fusion(f32[4,3,512,256]{3,2,1,0:T(8,128)S(1)} %fusion), kind=kOutput, calls=%fused_computation.146 | convolution fusion | flops 4831838208 | bytes 9437184 | tf_op jit(solution)/shard_map/hmrf,hmrg->hmfg/dot_general | solution.py:20
  473.4 4.1 multiply_add_fusion
  477.6 6.5 %subtract_convert_fusion = bf16[4,3,512,256]{3,2,0,1:T(8,128)(2,1)S(1)} fusion(f32[4,3,512,256]{3,2,0,1:T(8,128)S(1)} %bitcast.113, f32[4,3,256,256]{3,2,1,0:T(8,128)S(1)} %multiply_add_fusion, f32[4,3,512,256]{3,2,1,0:T(8,128)S(1)} %fusion), kind=kOutput, calls=%fused_computation.14 | convolution fusion | flops 4836556800 | bytes 18874368 | tf_op jit(solution)/shard_map/hmrf,hmfg->hmrg/dot_general | solution.py:34
  485.2 2.4 fusion.39
  487.5 1.2 copy.104
  (84 shorter events, 16.8 us)
Async XLA Ops:
  6.5 14.7 %copy-start.5 = (bf16[2,32,4096]{2,1,0:T(8,128)(2,1)S(1)}, bf16[2,32,4096]{2,1,0:T(8,128)(2,1)}, u32[]{:S(2)}) copy-start(bf16[2,32,4096]{2,1,0:T(8,128)(2,1)} %param.7) | copy-start | bytes 1572868
  6.5 67.2 %all-gather.2.cloned.1.call-start = ((), (), s32[]{:S(2)}) async-start(), calls=%async_computation.8 | async-start | bytes 6684672 | tf_op jit(solution)/shard_map/all_gather | solution.py:41
  9.7 8.0 %all-to-all-start = ((bf16[32,2,4]{0,2,1:T(4,128)(2,1)}), bf16[32,2,4]{0,2,1:T(4,128)(2,1)S(1)}, u32[]{:S(2)}, u32[]{:S(2)}) async-start(bf16[32,2,4]{0,2,1:T(4,128)(2,1)} %bitcast), calls=%async_computation | async-start | bytes 4096 | tf_op jit(solution)/shard_map/all_to_all | solution.py:50
  17.7 8.6 %all-to-all-start.2 = ((bf16[32,2,2048]{2,0,1:T(8,128)(2,1)}), bf16[32,2,2048]{2,0,1:T(8,128)(2,1)S(1)}, u32[]{:S(2)}, u32[]{:S(2)}) async-start(bf16[32,2,2048]{2,0,1:T(8,128)(2,1)} %copy.67), calls=%async_computation.2 | async-start | bytes 524288 | tf_op jit(solution)/shard_map/all_to_all | solution.py:48
  26.4 8.6 %all-to-all-start.1 = ((bf16[32,2,2048]{2,0,1:T(8,128)(2,1)}), bf16[32,2,2048]{2,0,1:T(8,128)(2,1)S(1)}, u32[]{:S(2)}, u32[]{:S(2)}) async-start(bf16[32,2,2048]{2,0,1:T(8,128)(2,1)} %copy.65), calls=%async_computation.1 | async-start | bytes 524288 | tf_op jit(solution)/shard_map/all_to_all | solution.py:49
  29.8 191.0 %all-reduce.3.cloned.1.call-start = ((), (), s32[]{:S(2)}) async-start(), calls=%async_computation.9 | async-start | bytes 12582912 | tf_op jit(solution)/shard_map/psum | solution.py:81
  82.6 6.8 %all-to-all-start.4 = ((bf16[32,2,4]{0,2,1:T(4,128)(2,1)}), bf16[32,2,4]{0,2,1:T(4,128)(2,1)S(1)}, u32[]{:S(2)}, u32[]{:S(2)}) async-start(bf16[32,2,4]{0,2,1:T(4,128)(2,1)} %bitcast.23), calls=%async_computation.4 | async-start | bytes 4096 | tf_op jit(solution)/shard_map/all_to_all | solution.py:50
  89.5 8.6 %all-to-all-start.5 = ((bf16[32,2,2048]{2,0,1:T(8,128)(2,1)}), bf16[32,2,2048]{2,0,1:T(8,128)(2,1)S(1)}, u32[]{:S(2)}, u32[]{:S(2)}) async-start(bf16[32,2,2048]{2,0,1:T(8,128)(2,1)} %copy.86), calls=%async_computation.5 | async-start | bytes 524288 | tf_op jit(solution)/shard_map/all_to_all | solution.py:49
  98.1 8.6 %all-to-all-start.6 = ((bf16[32,2,2048]{2,0,1:T(8,128)(2,1)}), bf16[32,2,2048]{2,0,1:T(8,128)(2,1)S(1)}, u32[]{:S(2)}, u32[]{:S(2)}) async-start(bf16[32,2,2048]{2,0,1:T(8,128)(2,1)} %copy.88), calls=%async_computation.6 | async-start | bytes 524288 | tf_op jit(solution)/shard_map/all_to_all | solution.py:48
  101.5 324.0 %all-reduce.5.cloned.1.call-start = ((), (), s32[]{:S(2)}) async-start(), calls=%async_computation.10 | async-start | bytes 12582912 | tf_op jit(solution)/shard_map/psum | solution.py:81
  220.8 25.5 %slice-start.4 = ((s8[6291456]{0:T(1024)(128)(4,1)}), s8[2097152]{0:T(1024)(128)(4,1)S(1)}, s32[]{:S(2)}) async-start(s8[6291456]{0:T(1024)(128)(4,1)} %bitcast.116), calls=%async_computation.15 | async-start | bytes 4194304
  239.9 6.4 %slice-start.5 = ((s8[6291456]{0:T(1024)(128)(4,1)}), s8[4194304]{0:T(1024)(128)(4,1)S(1)}, s32[]{:S(2)}) async-start(s8[6291456]{0:T(1024)(128)(4,1)} %bitcast.116), calls=%async_computation.16 | async-start | bytes 8388608
  239.9 6.4 %copy-start.1 = (f32[4,3,256,256]{3,2,1,0:T(8,128)S(1)}, f32[4,3,256,256]{3,2,1,0:T(8,128)}, u32[]{:S(2)}) copy-start(f32[4,3,256,256]{3,2,1,0:T(8,128)} %get-tuple-element.18) | copy-start | bytes 9437188
  239.9 31.8 %slice-start.2 = ((s8[6291456]{0:T(1024)(128)(4,1)}), s8[4194304]{0:T(1024)(128)(4,1)S(1)}, s32[]{:S(2)}) async-start(s8[6291456]{0:T(1024)(128)(4,1)} %bitcast.114), calls=%async_computation.13 | async-start | bytes 8388608
  246.4 25.4 %slice-start.3 = ((s8[6291456]{0:T(1024)(128)(4,1)}), s8[2097152]{0:T(1024)(128)(4,1)S(1)}, s32[]{:S(2)}) async-start(s8[6291456]{0:T(1024)(128)(4,1)} %bitcast.114), calls=%async_computation.14 | async-start | bytes 4194304
  271.8 8.1 %copy-start.2 = (bf16[64,4,512]{2,1,0:T(4,128)(2,1)S(1)}, bf16[64,4,512]{2,1,0:T(4,128)(2,1)}, u32[]{:S(2)}) copy-start(bf16[64,4,512]{2,1,0:T(4,128)(2,1)} %reshape.94) | copy-start | bytes 786436
  279.9 0.9 copy-start.4
  291.5 9.4 %all-to-all-start.3 = ((bf16[32,2,2048]{2,0,1:T(8,128)(2,1)}), bf16[32,2,2048]{2,0,1:T(8,128)(2,1)}, u32[]{:S(2)}, u32[]{:S(2)}) async-start(bf16[32,2,2048]{2,0,1:T(8,128)(2,1)} %copy.80), calls=%async_computation.3 | async-start | bytes 524288 | tf_op jit(solution)/shard_map/all_to_all | solution.py:47
  300.9 9.4 %all-to-all-start.7 = ((bf16[32,2,2048]{2,0,1:T(8,128)(2,1)}), bf16[32,2,2048]{2,0,1:T(8,128)(2,1)}, u32[]{:S(2)}, u32[]{:S(2)}) async-start(bf16[32,2,2048]{2,0,1:T(8,128)(2,1)} %copy.101), calls=%async_computation.7 | async-start | bytes 524288 | tf_op jit(solution)/shard_map/all_to_all | solution.py:47
  425.5 25.6 %slice-start.6 = ((s8[6291456]{0:T(1024)(128)(4,1)}), s8[2097152]{0:T(1024)(128)(4,1)S(1)}, s32[]{:S(2)}) async-start(s8[6291456]{0:T(1024)(128)(4,1)} %bitcast.118), calls=%async_computation.17 | async-start | bytes 4194304
  444.4 6.7 %slice-start.7 = ((s8[6291456]{0:T(1024)(128)(4,1)}), s8[4194304]{0:T(1024)(128)(4,1)S(1)}, s32[]{:S(2)}) async-start(s8[6291456]{0:T(1024)(128)(4,1)} %bitcast.118), calls=%async_computation.18 | async-start | bytes 8388608
  444.4 6.7 %copy-start = (f32[4,3,256,256]{3,2,1,0:T(8,128)S(1)}, f32[4,3,256,256]{3,2,1,0:T(8,128)}, u32[]{:S(2)}) copy-start(f32[4,3,256,256]{3,2,1,0:T(8,128)} %get-tuple-element.22) | copy-start | bytes 9437188
  444.4 33.2 %slice-start = ((s8[6291456]{0:T(1024)(128)(4,1)}), s8[4194304]{0:T(1024)(128)(4,1)S(1)}, s32[]{:S(2)}) async-start(s8[6291456]{0:T(1024)(128)(4,1)} %bitcast.112), calls=%async_computation.11 | async-start | bytes 8388608
  451.1 26.4 %slice-start.1 = ((s8[6291456]{0:T(1024)(128)(4,1)}), s8[2097152]{0:T(1024)(128)(4,1)S(1)}, s32[]{:S(2)}) async-start(s8[6291456]{0:T(1024)(128)(4,1)} %bitcast.112), calls=%async_computation.12 | async-start | bytes 4194304
  477.6 6.6 %copy-start.6 = (bf16[64,4,512]{2,1,0:T(4,128)(2,1)S(1)}, bf16[64,4,512]{2,1,0:T(4,128)(2,1)}, u32[]{:S(2)}) copy-start(bf16[64,4,512]{2,1,0:T(4,128)(2,1)} %reshape.95) | copy-start | bytes 786436
  484.1 4.7 copy-start.3
Sparse Core Ops, SparseCore 0:
  9.5 64.1 all-gather.1
  82.7 137.9 all-reduce.2
  286.1 139.3 all-reduce.4
where the time goes:
time: 502 us; the launch traced here: 497 us
  waiting for transfers between devices  285 us (57%)
  matrix products  130 us (26%)
  starting transfers between devices  29.8 us (6%)
  local copies, waits for them, and re-layouts  26.7 us (5%)
  between operations  14.1 us (3%)
  other arithmetic  11.8 us (2%)
    psum x2, waiting for transfers between devices, local(): total_grad = lax.psum(gradients, 'seq')  219 us
    dot_general x4, matrix products, local_gram(): jnp.einsum('hmrf,hmrg->hmfg', weight_matrices, weight_matrices, precision...  59.2 us
    all_gather x1, waiting for transfers between devices, local(): weights = lax.all_gather(fast_init, 'seq', axis=2, tiled=True)  38.2 us
    dot_general x4, matrix products, newton_schulz(): jnp.einsum('hmrf,hmfg->hmrg', current_weights, polynomial_update, precisi...  36.9 us
    dot_general x4, matrix products, newton_schulz(): jnp.einsum('hmfg,hmgk->hmfk', gram_matrix, gram_matrix, precision=FULL_PR...  21.1 us
  transfers between devices with their start and end apart: 11, of which 11 were waited for; matrix products, arithmetic and copies ran while one was open for 5% of the time, Pallas kernels for 0%

commit v1 on v0

--- a/solution.py
+++ b/solution.py
@@ -1,3 +1,4 @@
+import functools
 import jax
 import jax.numpy as jnp
 from jax import lax
@@ -9,6 +10,20 @@
 COEF_C = 2.0315
 LEARNING_STEP = 0.5
 FULL_PRECISION = lax.Precision.HIGHEST
+
+
+def expand_patches_on_mesh(vals, peer_axis):
+    parts_n = lax.axis_size(peer_axis)
+    then = vals
+    for idx in [t for t in (1, 2, 4, 8, 16) if t < parts_n]:
+        runs = []
+        for dev_i in tuple(range(parts_n)):
+            runs.append((dev_i, dev_i ^ idx))
+        then = then + lax.ppermute(then, peer_axis, runs)
+    return then
+
+
+write_the_object = functools.partial(expand_patches_on_mesh, peer_axis="seq")
 
 
 def silu_parts(gate_pre):
@@ -78,7 +93,7 @@
             ],
             axis=1,
         )
-        total_grad = lax.psum(gradients, "seq")
+        total_grad = write_the_object(gradients)
         update = newton_schulz(total_grad, local_gram)
         weights = weights - LEARNING_STEP * update
         low = weights.astype(jnp.bfloat16)

time: 502 us -> 1330 us (2.65)
  waiting for transfers between devices: 285 us -> 1120 us
  matrix products: 130 us -> 99.1 us
  other arithmetic: 11.8 us -> 36.1 us
    ppermute x0 -> x8, waiting for transfers between devices: none -> 1050 us  [expand_patches_on_mesh(): then = then + lax.ppermute(then, peer_axis, runs)]
    psum x2 -> x0, waiting for transfers between devices: 219 us -> none  [local(): total_grad = lax.psum(gradients, 'seq')]
    add x0 -> x8, other arithmetic: none -> 28.5 us  [expand_patches_on_mesh(): then = then + lax.ppermute(then, peer_axis, runs)]
    dot_general x4, matrix products: 59.2 us -> 33.6 us  [local_gram(): jnp.einsum('hmrf,hmrg->hmfg', weight_matrices, weight_matrices, precision...]
  transfers between devices with their start and end apart: 11 -> 17, of which waited for: 11 -> 17; matrix products, arithmetic and copies ran while one was open for 5% -> 2% of each run, Pallas kernels for 0% -> 0%
where the time goes in v1:
time: 1330 us
  waiting for transfers between devices  1120 us (84%)
  matrix products  99.1 us (7%)
  other arithmetic  36.1 us (3%)
  starting transfers between devices  36 us (3%)
  local copies, waits for them, and re-layouts  25.7 us (2%)
  between operations  14.4 us (1%)
    ppermute x8, waiting for transfers between devices, expand_patches_on_mesh(): then = then + lax.ppermute(then, peer_axis, runs)  1050 us
    all_gather x1, waiting for transfers between devices, local(): weights = lax.all_gather(fast_init, 'seq', axis=2, tiled=True)  38.3 us
    dot_general x4, matrix products, newton_schulz(): jnp.einsum('hmrf,hmfg->hmrg', current_weights, polynomial_update, precisi...  36.5 us
    dot_general x4, matrix products, local_gram(): jnp.einsum('hmrf,hmrg->hmfg', weight_matrices, weight_matrices, precision...  33.6 us
    add x8, other arithmetic, expand_patches_on_mesh(): then = then + lax.ppermute(then, peer_axis, runs)  28.5 us
  transfers between devices with their start and end apart: 17, of which 17 were waited for; matrix products, arithmetic and copies ran while one was open for 2% of the time, Pallas kernels for 0%

profile of v1, /device:TPU:0, one launch (start us, length us, event | category | flops | bytes accessed | tf_op | source)
XLA Modules:
  0.0 1326.3 jit_solution(11506815579728361066)
XLA Ops:
  9.7 4.3 all-to-all-start
  17.6 3.5 all-to-all-start.2
  22.1 4.1 all-to-all-done.2
  26.2 3.4 all-to-all-start.1
  29.9 4.9 all-to-all-done.1
  35.4 38.3 %all-gather.2.cloned.1.call-done = f32[4,3,512,256]{3,2,0,1:T(8,128)} async-done(((f32[4,3,32,256]{3,2,0,1:T(8,128)}), f32[4,3,512,256]{3,2,0,1:T(8,128)}) %all-gather.2.cloned.1.call-update) | async-done | bytes 6291472 | tf_op jit(solution)/shard_map/all_gather | solution.py:56
  73.7 3.1 convert_element_type.105
  80.3 9.9 collective-permute-done
  92.4 137.1 %collective-permute-done.1 = f32[4,3,512,256]{2,3,0,1:T(8,128)S(1)} collective-permute-done((f32[4,3,512,256]{2,3,0,1:T(8,128)S(1)}, f32[4,3,512,256]{2,3,0,1:T(8,128)S(1)}, u32[]{:S(2)}, u32[]{:S(2)}) %collective-permute-start.1) | collective-permute-done | bytes 6291488 | tf_op jit(solution)/shard_map/ppermute | solution.py:22
  229.5 2.3 fusion.114
  233.5 135.3 %collective-permute-done.2 = f32[4,3,512,256]{2,3,0,1:T(8,128)S(1)} collective-permute-done((f32[4,3,512,256]{2,3,0,1:T(8,128)S(1)}, f32[4,3,512,256]{2,3,0,1:T(8,128)S(1)}, u32[]{:S(2)}, u32[]{:S(2)}) %collective-permute-start.2) | collective-permute-done | bytes 6291488 | tf_op jit(solution)/shard_map/ppermute | solution.py:22
  368.8 4.2 add.110
  373.0 1.9 collective-permute-start.3
  374.9 3.2 all-to-all-start.4
  381.9 3.4 all-to-all-start.5
  385.4 5.1 all-to-all-done.5
  390.5 3.7 all-to-all-start.6
  394.5 4.7 all-to-all-done.6
  401.1 243.9 %collective-permute-done.3 = f32[4,3,512,256]{2,3,0,1:T(8,128)} collective-permute-done((f32[4,3,512,256]{2,3,0,1:T(8,128)}, f32[4,3,512,256]{2,3,0,1:T(8,128)}, u32[]{:S(2)}, u32[]{:S(2)}) %collective-permute-start.3) | collective-permute-done | bytes 6291488 | tf_op jit(solution)/shard_map/ppermute | solution.py:22
  645.0 6.2 add.111
  651.2 6.2 select_reduce_fusion.1
  657.5 4.2 fusion.36
  661.7 10.6 fusion.2
  672.4 10.4 fusion.103
  682.8 4.1 multiply_add_fusion.1
  686.9 8.1 fusion.102
  698.6 10.1 collective-permute-done.4
  710.8 137.0 %collective-permute-done.5 = f32[4,3,512,256]{2,3,0,1:T(8,128)S(1)} collective-permute-done((f32[4,3,512,256]{2,3,0,1:T(8,128)S(1)}, f32[4,3,512,256]{2,3,0,1:T(8,128)S(1)}, u32[]{:S(2)}, u32[]{:S(2)}) %collective-permute-start.5) | collective-permute-done | bytes 6291488 | tf_op jit(solution)/shard_map/ppermute | solution.py:22
  847.9 2.3 fusion.113
  850.3 136.7 %collective-permute-done.6 = f32[4,3,512,256]{2,3,0,1:T(8,128)S(1)} collective-permute-done((f32[4,3,512,256]{2,3,0,1:T(8,128)S(1)}, f32[4,3,512,256]{2,3,0,1:T(8,128)S(1)}, u32[]{:S(2)}, u32[]{:S(2)}) %collective-permute-start.6) | collective-permute-done | bytes 6291488 | tf_op jit(solution)/shard_map/ppermute | solution.py:22
  987.0 4.2 add.123
  992.8 1.9 all_to_all.95
  996.4 4.1 all-to-all-start.3
  1000.5 1.9 all_to_all.105
  1005.8 4.5 all-to-all-start.7
  1010.3 1.9 reshape.93
  1012.2 3.4 all-to-all-done.7
  1017.4 2.0 convolution_bitcast_fusion.12
  1019.4 2.4 fusion.38
  1023.8 239.3 %collective-permute-done.7 = f32[4,3,512,256]{2,3,0,1:T(8,128)} collective-permute-done((f32[4,3,512,256]{2,3,0,1:T(8,128)}, f32[4,3,512,256]{2,3,0,1:T(8,128)}, u32[]{:S(2)}, u32[]{:S(2)}) %collective-permute-start.7) | collective-permute-done | bytes 6291488 | tf_op jit(solution)/shard_map/ppermute | solution.py:22
  1263.1 6.2 add.124
  1269.3 6.2 select_reduce_fusion
  1275.6 3.9 fusion.37
  1279.6 11.2 fusion
  1290.8 10.8 fusion.104
  1301.6 4.4 multiply_add_fusion
  1306.0 6.5 subtract_convert_fusion
  1313.6 2.3 fusion.39
  (96 shorter events, 42.5 us)
Async XLA Ops:
  6.5 14.5 %copy-start.6 = (bf16[2,32,4096]{2,1,0:T(8,128)(2,1)S(1)}, bf16[2,32,4096]{2,1,0:T(8,128)(2,1)}, u32[]{:S(2)}) copy-start(bf16[2,32,4096]{2,1,0:T(8,128)(2,1)} %param.7) | copy-start | bytes 1572868
  6.5 67.2 %all-gather.2.cloned.1.call-start = ((), (), s32[]{:S(2)}) async-start(), calls=%async_computation.8 | async-start | bytes 6684672 | tf_op jit(solution)/shard_map/all_gather | solution.py:56
  9.7 7.9 all-to-all-start
  17.6 8.6 all-to-all-start.2
  26.2 8.6 all-to-all-start.1
  80.0 10.2 collective-permute-start
  91.8 137.8 %collective-permute-start.1 = (f32[4,3,512,256]{2,3,0,1:T(8,128)S(1)}, f32[4,3,512,256]{2,3,0,1:T(8,128)S(1)}, u32[]{:S(2)}, u32[]{:S(2)}) collective-permute-start(f32[4,3,512,256]{2,3,0,1:T(8,128)S(1)} %fusion.97), channel_id=1, source_target_pairs={{0,4},{2,6},{4,0},{6,2},{8,12},{10,14},{12,8},{14,10},{16,20},{18,... | collective-permute-start | bytes 18874376 | tf_op jit(solution)/shard_map/ppermute | solution.py:22
  231.9 136.9 %collective-permute-start.2 = (f32[4,3,512,256]{2,3,0,1:T(8,128)S(1)}, f32[4,3,512,256]{2,3,0,1:T(8,128)S(1)}, u32[]{:S(2)}, u32[]{:S(2)}) collective-permute-start(f32[4,3,512,256]{2,3,0,1:T(8,128)S(1)} %fusion.114), channel_id=1, source_target_pairs={{0,8},{2,10},{4,12},{6,14},{8,0},{10,2},{12,4},{14,6},{16,24},{18,... | collective-permute-start | bytes 18874376 | tf_op jit(solution)/shard_map/ppermute | solution.py:22
  373.0 272.0 %collective-permute-start.3 = (f32[4,3,512,256]{2,3,0,1:T(8,128)}, f32[4,3,512,256]{2,3,0,1:T(8,128)}, u32[]{:S(2)}, u32[]{:S(2)}) collective-permute-start(f32[4,3,512,256]{2,3,0,1:T(8,128)} %add.110), channel_id=1, source_target_pairs={{0,16},{2,18},{4,20},{6,22},{8,24},{10,26},{12,28},{14,30},{16,0},... | collective-permute-start | bytes 18874376 | tf_op jit(solution)/shard_map/ppermute | solution.py:22
  374.9 6.9 all-to-all-start.4
  381.9 8.6 all-to-all-start.5
  390.5 8.8 all-to-all-start.6
  651.2 6.2 copy-start.2
  657.5 4.2 copy-start.3
  657.5 29.4 %slice-start.2 = ((s8[6291456]{0:T(1024)(128)(4,1)}), s8[4194304]{0:T(1024)(128)(4,1)S(1)}, s32[]{:S(2)}) async-start(s8[6291456]{0:T(1024)(128)(4,1)} %bitcast.114), calls=%async_computation.11 | async-start | bytes 8388608
  661.7 25.2 %slice-start.3 = ((s8[6291456]{0:T(1024)(128)(4,1)}), s8[2097152]{0:T(1024)(128)(4,1)S(1)}, s32[]{:S(2)}) async-start(s8[6291456]{0:T(1024)(128)(4,1)} %bitcast.114), calls=%async_computation.12 | async-start | bytes 4194304
  686.9 8.1 copy-start.4
  695.0 0.9 copy-start.5
  698.5 10.2 collective-permute-start.4
  710.3 137.6 %collective-permute-start.5 = (f32[4,3,512,256]{2,3,0,1:T(8,128)S(1)}, f32[4,3,512,256]{2,3,0,1:T(8,128)S(1)}, u32[]{:S(2)}, u32[]{:S(2)}) collective-permute-start(f32[4,3,512,256]{2,3,0,1:T(8,128)S(1)} %fusion.96), channel_id=1, source_target_pairs={{0,4},{2,6},{4,0},{6,2},{8,12},{10,14},{12,8},{14,10},{16,20},{18,... | collective-permute-start | bytes 18874376 | tf_op jit(solution)/shard_map/ppermute | solution.py:22
  850.2 141.8 %copy-start.7 = (bf16[2,32,4096]{2,1,0:T(8,128)(2,1)S(1)}, bf16[2,32,4096]{2,1,0:T(8,128)(2,1)}, u32[]{:S(2)}) copy-start(bf16[2,32,4096]{2,1,0:T(8,128)(2,1)} %param.5) | copy-start | bytes 1572868
  850.2 136.8 %collective-permute-start.6 = (f32[4,3,512,256]{2,3,0,1:T(8,128)S(1)}, f32[4,3,512,256]{2,3,0,1:T(8,128)S(1)}, u32[]{:S(2)}, u32[]{:S(2)}) collective-permute-start(f32[4,3,512,256]{2,3,0,1:T(8,128)S(1)} %fusion.113), channel_id=1, source_target_pairs={{0,8},{2,10},{4,12},{6,14},{8,0},{10,2},{12,4},{14,6},{16,24},{18,... | collective-permute-start | bytes 18874376 | tf_op jit(solution)/shard_map/ppermute | solution.py:22
  991.2 271.9 %collective-permute-start.7 = (f32[4,3,512,256]{2,3,0,1:T(8,128)}, f32[4,3,512,256]{2,3,0,1:T(8,128)}, u32[]{:S(2)}, u32[]{:S(2)}) collective-permute-start(f32[4,3,512,256]{2,3,0,1:T(8,128)} %add.123), channel_id=1, source_target_pairs={{0,16},{2,18},{4,20},{6,22},{8,24},{10,26},{12,28},{14,30},{16,0},... | collective-permute-start | bytes 18874376 | tf_op jit(solution)/shard_map/ppermute | solution.py:22
  996.4 9.4 all-to-all-start.3
  1005.8 9.7 all-to-all-start.7
  1269.3 6.2 copy-start
  1275.6 3.9 copy-start.1
  1275.6 30.4 %slice-start = ((s8[6291456]{0:T(1024)(128)(4,1)}), s8[4194304]{0:T(1024)(128)(4,1)S(1)}, s32[]{:S(2)}) async-start(s8[6291456]{0:T(1024)(128)(4,1)} %bitcast.112), calls=%async_computation.9 | async-start | bytes 8388608
  1279.6 26.4 %slice-start.1 = ((s8[6291456]{0:T(1024)(128)(4,1)}), s8[2097152]{0:T(1024)(128)(4,1)S(1)}, s32[]{:S(2)}) async-start(s8[6291456]{0:T(1024)(128)(4,1)} %bitcast.112), calls=%async_computation.10 | async-start | bytes 4194304
  1306.0 6.6 copy-start.8
Sparse Core Ops, SparseCore 0:
  9.5 64.1 all-gather.1
